TPU v7x, 32 devices: a whole 2x2x4 slice. The times are simulated.
32 devices in a mesh: ens: 2 (over y), comp: 4 (over z), lat: 2 (over x), lon: 2 (over core).
Axes of the slice: x: 2, y: 2, z: 4, core: 2. Of those that a mesh axis runs over, the one named last changes fastest.
Arguments:
- spectrum: float32 [2304, 16, 256], P(('ens', 'comp'), 'lat', 'lon'), parts along dimension 0, may hold values from 0 to 2
- sea_mask: int32 [16, 256], P('lat', 'lon'), may hold values 0 or 1
- depth_class: int32 [16, 256], P('lat', 'lon'), may hold values from 0 to 15
- current_class: int32 [16, 256], P('lat', 'lon'), may hold values from 0 to 15
- speed_table: float32 [16, 32], replicated, may hold values from 0.1 to 0.5
- current_table: float32 [16, 2], replicated, may hold values from -0.14 to 0.14
- coupling: float32 [1152], replicated, may hold values from 0.05 to 0.5
- quad_index: int32 [2, 1152, 4], replicated, may hold values from 0 to 1151, as said below
- quad_weight: float32 [2, 1152, 4], replicated, may hold values from 0 to 1, as said below
Outputs:
- spectrum_out: float32 [2304, 16, 256], P(('ens', 'comp'), 'lat', 'lon'), parts along dimension 0
There are 2 independent parts, one for each index of `ens`. A program takes and returns all parts, laid end to end along the dimension named above; an argument that names none is the same for every part. Nothing has to cross between parts.
Inputs may be any that keep to these rules, and one draw needn't show every extreme that they name: `quad_index`: for each side (0 plus, 1 minus) and component k the four entries are distinct components: two adjacent frequencies crossed with two adjacent directions, directions counted modulo 36; a component's number is its frequency times 36 plus its direction. `quad_weight`: the four weights of each side and component are non-negative and sum to one.
All inputs are finite; a program needn't handle non-finite values. No bound on the sum of `sea_mask` on one device may be relied on, other than what follows from the above.
Results may differ from a plain program's by a relative error of at most 0.002.
Values sent between devices are 32-bit elements; how exact they have to be, the bound alone decides.
A program may use at most 64 MiB of HBM per device.

v0:
```python
import math

import jax
import jax.numpy as jnp
from jax import lax
from jax.sharding import PartitionSpec as P

NDIR = 36
SUBSTEPS = 4


plus_factor = 0.4096
minus_factor = 3.160494
cross_factor = 2.007843


def with_halo(block, sides, width):
    for axis, dim in sides:
        count = lax.axis_size(axis)
        forward = [(i, i + 1) for i in range(count - 1)]
        forward.append((count - 1, 0))
        backward = [(target, source) for source, target in forward]
        low = lax.ppermute(
            lax.slice_in_dim(block, block.shape[dim] - width, None, axis=dim), axis, forward
        )
        high = lax.ppermute(lax.slice_in_dim(block, 0, width, axis=dim), axis, backward)
        block = jnp.concatenate([low, block, high], axis=dim)
    return block


def minmod(former, latter):
    return jnp.maximum(0.0, jnp.minimum(former, latter)) + jnp.minimum(
        0.0, jnp.maximum(former, latter)
    )


def part_of(array, start, length, axis):
    return lax.slice_in_dim(array, start, start + length, axis=axis)


def face_flux(energy, cour, wet_cells, axis):
    length = energy.shape[axis]
    differences = part_of(energy, 1, length - 1, axis) - part_of(energy, 0, length - 1, axis)
    slopes = minmod(
        part_of(differences, 1, length - 2, axis), part_of(differences, 0, length - 2, axis)
    )
    face_count = length - 3
    face_speed = (
        0.5
        * (part_of(cour, 1, face_count, axis) + part_of(cour, 2, face_count, axis))
        * (part_of(wet_cells, 1, face_count, axis) * part_of(wet_cells, 2, face_count, axis))
    )
    upwind_left = part_of(energy, 1, face_count, axis) + 0.5 * (1.0 - face_speed) * part_of(
        slopes, 0, face_count, axis
    )
    upwind_right = part_of(energy, 2, face_count, axis) - 0.5 * (1.0 + face_speed) * part_of(
        slopes, 1, face_count, axis
    )
    return jnp.maximum(face_speed, 0.0) * upwind_left + jnp.minimum(face_speed, 0.0) * upwind_right


def advance(energy, cour_x, cour_y, wet_cells):
    flux_lon = face_flux(energy[:, 2:-2, :], cour_x[:, 2:-2, :], wet_cells[:, 2:-2, :], 2)
    flux_lat = face_flux(energy[:, :, 2:-2], cour_y[:, :, 2:-2], wet_cells[:, :, 2:-2], 1)
    return (
        energy[:, 2:-2, 2:-2]
        - (flux_lon[:, :, 1:] - flux_lon[:, :, :-1])
        - (flux_lat[:, 1:, :] - flux_lat[:, :-1, :])
    )


def courant(comp_ids, depth_grid, current_grid, speed_table, current_table):
    n_depth, n_freq = speed_table.shape
    n_current = current_table.shape[0]
    depth_hot = (depth_grid[None] == jnp.arange(n_depth, dtype=jnp.int32)[:, None, None]).astype(
        jnp.float32
    )
    current_hot = (
        current_grid[None] == jnp.arange(n_current, dtype=jnp.int32)[:, None, None]
    ).astype(jnp.float32)
    freq_hot = ((comp_ids // NDIR)[:, None] == jnp.arange(n_freq, dtype=jnp.int32)[None, :]).astype(
        jnp.float32
    )
    comp_speed = jnp.dot(freq_hot, speed_table.T, precision=lax.Precision.HIGHEST)
    speeds = jnp.einsum("kn,nhw->khw", comp_speed, depth_hot, precision=lax.Precision.HIGHEST)
    current_uv = jnp.einsum(
        "nc,nhw->chw", current_table, current_hot, precision=lax.Precision.HIGHEST
    )
    angles = 2.0 * math.pi / NDIR * (comp_ids % NDIR).astype(jnp.float32)
    cour_x = speeds * jnp.cos(angles)[:, None, None] + current_uv[0]
    cour_y = speeds * jnp.sin(angles)[:, None, None] + current_uv[1]
    return (cour_x, cour_y)


def dense_kernel(table_index, table_weight):
    comp_total = table_index.shape[0]
    columns = jnp.arange(comp_total, dtype=jnp.int32)[None, :]
    weights = table_weight.astype(jnp.bfloat16)
    kernel = jnp.where(columns == table_index[:, 3:4], weights[:, 3:4], jnp.zeros((), jnp.bfloat16))
    for corner in (2, 1, 0):
        kernel = jnp.where(
            columns == table_index[:, corner : corner + 1], weights[:, corner : corner + 1], kernel
        )
    return kernel


def interact(energy, kernel_plus, kernel_minus, coupling):
    energy_low = energy.astype(jnp.bfloat16)
    plus_side = jnp.dot(kernel_plus, energy_low, preferred_element_type=jnp.float32)
    minus_side = jnp.dot(kernel_minus, energy_low, preferred_element_type=jnp.float32)
    source = coupling[:, None] * (
        energy * energy * (plus_factor * plus_side + minus_factor * minus_side)
        - cross_factor * energy * plus_side * minus_side
    )
    source_low = source.astype(jnp.bfloat16)
    contract = (((0,), (0,)), ((), ()))
    net_gain = (
        lax.dot_general(kernel_plus, source_low, contract, preferred_element_type=jnp.float32)
        + lax.dot_general(kernel_minus, source_low, contract, preferred_element_type=jnp.float32)
        - 2.0 * source
    )
    return energy + net_gain / (1.0 + jnp.abs(net_gain))


def window(array, offset):
    return array[:, offset : array.shape[1] - offset, offset : array.shape[2] - offset]


def local(
    spectrum,
    sea_mask,
    depth_class,
    current_class,
    speed_table,
    current_table,
    coupling,
    quad_index,
    quad_weight,
):
    comps_local, lat_rows, lon_cols = spectrum.shape
    n_comp = lax.axis_size("comp")
    n_lat = lax.axis_size("lat")
    deep_rim = 2 * SUBSTEPS
    stacked = jnp.stack([sea_mask, depth_class, current_class])
    padded = with_halo(stacked, (("lat", 1), ("lon", 2)), deep_rim)
    row_global = (
        lax.axis_index("lat") * lat_rows
        - deep_rim
        + jnp.arange(lat_rows + 2 * deep_rim, dtype=jnp.int32)
    )
    inside = ((row_global >= 0) & (row_global < lat_rows * n_lat)).astype(jnp.float32)[:, None]
    wet_rim = (padded[0].astype(jnp.float32) * inside)[None]
    comp_ids = lax.axis_index("comp") * comps_local + jnp.arange(comps_local, dtype=jnp.int32)
    cour_x, cour_y = courant(comp_ids, padded[1], padded[2], speed_table, current_table)
    energy = spectrum * sea_mask.astype(jnp.float32)[None]
    inner_rows = inside[deep_rim - 2 : deep_rim + lat_rows + 2]
    offset = deep_rim - 2
    for substep in range(SUBSTEPS):
        rimmed = with_halo(energy, (("lat", 1), ("lon", 2)), 2) * inner_rows[None]
        energy = advance(
            rimmed, window(cour_x, offset), window(cour_y, offset), window(wet_rim, offset)
        )
    kernel_plus = dense_kernel(quad_index[0], quad_weight[0])
    kernel_minus = dense_kernel(quad_index[1], quad_weight[1])
    cell_count = lat_rows * lon_cols
    outgoing = energy.reshape(comps_local, n_comp, cell_count // n_comp)
    pieces = lax.all_to_all(outgoing, "comp", split_axis=1, concat_axis=0, tiled=True)
    point_grid = pieces.reshape(pieces.shape[0], pieces.shape[2])
    arrived = interact(point_grid, kernel_plus, kernel_minus, coupling).reshape(pieces.shape)
    returned = lax.all_to_all(arrived, "comp", split_axis=0, concat_axis=1, tiled=True)
    return returned.reshape(comps_local, lat_rows, lon_cols)


def solution(mesh):
    placed = (
        P(("ens", "comp"), "lat", "lon"),
        P("lat", "lon"),
        P("lat", "lon"),
        P("lat", "lon"),
        P(),
        P(),
        P(),
        P(),
        P(),
    )
    return jax.shard_map(
        local,
        mesh=mesh,
        in_specs=placed,
        out_specs=P(("ens", "comp"), "lat", "lon"),
        check_vma=False,
    )
```

profile of v0, /device:TPU:0, one launch (start us, length us, event | category | flops | bytes accessed | tf_op | source)
XLA Modules:
  0.0 197.4 jit_solution(13081938902043382700)
XLA Ops:
  0.0 0.7 pad_add_fusion.2
  0.7 3.0 %collective-permute-start.4 = (s32[3,8,128]{2,1,0:T(8,128)S(1)}, s32[3,8,128]{2,1,0:T(8,128)S(1)}, u32[]{:S(2)}, u32[]{:S(2)}) collective-permute-start(s32[3,8,128]{2,1,0:T(8,128)S(1)} %pad_add_fusion.2), channel_id=1, source_target_pairs={{0,2},{2,0},{1,3},{3,1},{4,6},{6,4},{5,7},{7,5},{8,10},{10,8},{9,1... | collective-permute-start | bytes 36872 | tf_op jit(solution)/shard_map/ppermute | solution.py:23
  3.7 0.7 convert_element_type.41
  4.4 1.7 copy.13
  6.5 2.1 %collective-permute-start = (f32[288,2,128]{0,2,1:T(8,128)S(1)}, f32[288,2,128]{0,2,1:T(8,128)S(1)}, u32[]{:S(2)}, u32[]{:S(2)}) collective-permute-start(f32[288,2,128]{0,2,1:T(8,128)S(1)} %get-tuple-element.41), channel_id=1, source_target_pairs={{0,2},{2,0},{1,3},{3,1},{4,6},{6,4},{5,7},{7,5},{8,10},{10,8},{9,1... | collective-permute-start | bytes 884744 | tf_op jit(solution)/shard_map/ppermute | solution.py:23
  9.1 0.5 collective-permute-start.7
  9.7 0.6 collective-permute-done.6
  10.9 3.2 %multiply_add_fusion.1 = (f32[288,24,144]{0,2,1:T(8,128)S(1)}, f32[288,24,144]{0,2,1:T(8,128)S(1)}) fusion(f32[24,144]{1,0:T(8,128)S(1)} %get-tuple-element.62, f32[288]{0:T(512)S(1)} %get-tuple-element.64, f32[24,144]{1,0:T(8,128)S(1)} %get-tuple-element.61, f32[288]{0:T(512)S(1)} %get-tuple-element.63, f32[288,16,1]{0,1,2:T(8,128)S(1)} %convolution_bitcast_fusion.1, ...), kind=kOutput, calls=%fused_computation.9 | convolution fusion | flops 195139584 | bytes 8024832 | tf_op jit(solution)/shard_map/kn,nhw->khw/dot_general | solution.py:85
  14.3 4.2 %collective-permute-done = f32[288,2,128]{0,2,1:T(8,128)S(1)} collective-permute-done((f32[288,2,128]{0,2,1:T(8,128)S(1)}, f32[288,2,128]{0,2,1:T(8,128)S(1)}, u32[]{:S(2)}, u32[]{:S(2)}) %collective-permute-start) | collective-permute-done | bytes 294944 | tf_op jit(solution)/shard_map/ppermute | solution.py:23
  18.5 7.0 %collective-permute-done.1 = f32[288,2,128]{0,2,1:T(8,128)S(1)} collective-permute-done((f32[288,2,128]{0,2,1:T(8,128)S(1)}, f32[288,2,128]{0,2,1:T(8,128)S(1)}, u32[]{:S(2)}, u32[]{:S(2)}) %collective-permute-start.1) | collective-permute-done | bytes 294944 | tf_op jit(solution)/shard_map/ppermute | solution.py:26
  25.7 0.5 collective-permute-start.3
  26.2 0.6 collective-permute-done.2
  27.0 0.3 maximum_multiply_fusion
  27.8 0.4 minimum_add_fusion.7
  28.2 0.3 minimum_add_fusion.3
  28.5 1.4 fusion.47
  30.0 1.6 fusion.26
  31.6 0.4 fusion.57
  32.1 1.8 collective-permute-start.8
  33.9 0.3 collective-permute-start.9
  34.2 10.0 %collective-permute-done.8 = f32[288,2,128]{0,2,1:T(8,128)S(1)} collective-permute-done((f32[288,2,128]{0,2,1:T(8,128)S(1)}, f32[288,2,128]{0,2,1:T(8,128)S(1)}, u32[]{:S(2)}, u32[]{:S(2)}) %collective-permute-start.8) | collective-permute-done | bytes 294944 | tf_op jit(solution)/shard_map/ppermute | solution.py:23
  44.1 7.8 %collective-permute-done.9 = f32[288,2,128]{0,2,1:T(8,128)S(1)} collective-permute-done((f32[288,2,128]{0,2,1:T(8,128)S(1)}, f32[288,2,128]{0,2,1:T(8,128)S(1)}, u32[]{:S(2)}, u32[]{:S(2)}) %collective-permute-start.9) | collective-permute-done | bytes 294944 | tf_op jit(solution)/shard_map/ppermute | solution.py:26
  52.0 0.5 collective-permute-start.11
  52.5 0.7 collective-permute-done.10
  53.4 0.3 maximum_multiply_fusion.1
  54.2 0.4 minimum_add_fusion.6
  54.6 0.3 minimum_add_fusion.2
  54.9 1.0 fusion.42
  56.0 0.9 fusion.21
  56.8 0.4 fusion.55
  57.3 1.8 collective-permute-start.12
  59.1 0.3 collective-permute-start.13
  59.4 10.0 %collective-permute-done.12 = f32[288,2,128]{0,2,1:T(8,128)S(1)} collective-permute-done((f32[288,2,128]{0,2,1:T(8,128)S(1)}, f32[288,2,128]{0,2,1:T(8,128)S(1)}, u32[]{:S(2)}, u32[]{:S(2)}) %collective-permute-start.12) | collective-permute-done | bytes 294944 | tf_op jit(solution)/shard_map/ppermute | solution.py:23
  69.4 7.8 %collective-permute-done.13 = f32[288,2,128]{0,2,1:T(8,128)S(1)} collective-permute-done((f32[288,2,128]{0,2,1:T(8,128)S(1)}, f32[288,2,128]{0,2,1:T(8,128)S(1)}, u32[]{:S(2)}, u32[]{:S(2)}) %collective-permute-start.13) | collective-permute-done | bytes 294944 | tf_op jit(solution)/shard_map/ppermute | solution.py:26
  77.3 0.5 collective-permute-start.15
  77.8 0.7 collective-permute-done.14
  78.6 0.3 maximum_multiply_fusion.2
  79.4 0.4 minimum_add_fusion.5
  79.8 1.0 fusion.37
  80.8 0.3 minimum_add_fusion.1
  81.2 0.9 fusion.16
  82.1 0.4 fusion.53
  82.5 1.8 collective-permute-start.16
  84.6 10.0 %collective-permute-done.16 = f32[288,2,128]{0,2,1:T(8,128)S(1)} collective-permute-done((f32[288,2,128]{0,2,1:T(8,128)S(1)}, f32[288,2,128]{0,2,1:T(8,128)S(1)}, u32[]{:S(2)}, u32[]{:S(2)}) %collective-permute-start.16) | collective-permute-done | bytes 294944 | tf_op jit(solution)/shard_map/ppermute | solution.py:23
  94.6 7.8 %collective-permute-done.17 = f32[288,2,128]{0,2,1:T(8,128)S(1)} collective-permute-done((f32[288,2,128]{0,2,1:T(8,128)S(1)}, f32[288,2,128]{0,2,1:T(8,128)S(1)}, u32[]{:S(2)}, u32[]{:S(2)}) %collective-permute-start.17) | collective-permute-done | bytes 294944 | tf_op jit(solution)/shard_map/ppermute | solution.py:26
  102.5 0.5 collective-permute-start.19
  103.0 0.7 collective-permute-done.18
  103.9 0.3 maximum_multiply_fusion.3
  104.6 0.4 minimum_add_fusion.4
  105.0 1.0 fusion.32
  106.1 0.5 minimum_add_fusion
  106.6 0.9 fusion.11
  107.5 0.4 fusion.51
  107.9 1.5 copy.14
  109.4 5.2 %all-to-all-start = ((f32[288,4,256]{2,0,1:T(8,128)}), f32[288,4,256]{2,0,1:T(8,128)S(1)}, u32[]{:S(2)}, u32[]{:S(2)}) async-start(f32[288,4,256]{2,0,1:T(8,128)} %copy.14), calls=%async_computation | async-start | bytes 2359296 | tf_op jit(solution)/shard_map/all_to_all | solution.py:167
  114.9 28.8 %all-to-all-done = f32[288,4,256]{2,0,1:T(8,128)S(1)} async-done(((f32[288,4,256]{2,0,1:T(8,128)}), f32[288,4,256]{2,0,1:T(8,128)S(1)}, u32[]{:S(2)}, u32[]{:S(2)}) %all-to-all-start) | async-done | bytes 1179680 | tf_op jit(solution)/shard_map/all_to_all | solution.py:167
  143.7 4.3 %fusion.72 = f32[1152,256]{1,0:T(8,128)S(1)} fusion(bf16[1152,256]{1,0:T(8,128)(2,1)S(1)} %bitcast_convert_fusion, s32[1152]{0:T(1024)S(1)} %get-tuple-element.55, s32[1152]{0:T(1024)S(1)} %get-tuple-element.54, s32[1152]{0:T(1024)S(1)} %get-tuple-element.53, s32[1152]{0:T(1024)S(1)} %get-tuple-element.56, bf16[1152]{0:T(1024)(128)(2,1)S(1)} %get-tuple-element.59, ...), kind=kOutput, calls=%fused_computation.132 | convolution fusion | flops 690094080 | bytes 1797120 | tf_op jit(solution)/shard_map/dot_general | solution.py:109
  148.1 4.6 %fusion.61 = f32[1152,256]{1,0:T(8,128)S(1)} fusion(f32[288,4,256]{2,0,1:T(8,128)S(1)} %all-to-all-done, f32[1152,256]{1,0:T(8,128)S(1)} %fusion.72, bf16[1152,256]{1,0:T(8,128)(2,1)S(1)} %bitcast_convert_fusion, s32[1152]{0:T(1024)S(1)} %get-tuple-element.6, s32[1152]{0:T(1024)S(1)} %get-tuple-element.7, s32[1152]{0:T(1024)S(1)} %get-tuple-element.8, ...), kind=kOutput, calls=%fused_computation.126 | convolution fusion | flops 693043200 | bytes 4161024 | tf_op jit(solution)/shard_map/dot_general | solution.py:110
  152.7 3.4 %fusion.70 = f32[1152,256]{1,0:T(8,128)S(1)} fusion(s32[1152]{0:T(1024)S(1)} %get-tuple-element.55, s32[1152]{0:T(1024)S(1)} %get-tuple-element.54, s32[1152]{0:T(1024)S(1)} %get-tuple-element.53, s32[1152]{0:T(1024)S(1)} %get-tuple-element.56, bf16[1152]{0:T(1024)(128)(2,1)S(1)} %get-tuple-element.59, bf16[1152]{0:T(1024)(128)(2,1)S(1)} %get-tuple-element.58, ...), kind=kOutput, calls=%fused_computation.131 | convolution fusion | flops 690388992 | bytes 2386944 | tf_op jit(solution)/shard_map/dot_general | solution.py:118
  156.1 3.6 %fusion.64 = f32[1152,1,256]{2,0,1:T(8,128)S(1)} fusion(f32[1152,256]{1,0:T(8,128)S(1)} %fusion.70, f32[288,4,256]{2,0,1:T(8,128)S(1)} %all-to-all-done, f32[1152,256]{1,0:T(8,128)S(1)} %fusion.61, s32[1152]{0:T(1024)S(1)} %get-tuple-element.6, s32[1152]{0:T(1024)S(1)} %get-tuple-element.7, s32[1152]{0:T(1024)S(1)} %get-tuple-element.8, ...), kind=kOutput, calls=%fused_computation.129 | convolution fusion | flops 692453376 | bytes 4746240 | tf_op jit(solution)/shard_map/dot_general | solution.py:119
  159.6 4.9 %copy.15 = f32[1152,1,256]{2,1,0:T(1,128)S(1)} copy(f32[1152,1,256]{2,0,1:T(8,128)S(1)} %fusion.64) | data formatting | bytes 2359296 | tf_op jit(solution)/shard_map/reshape | solution.py:169
  164.5 30.6 %all_to_all.30 = f32[1152,1,256]{2,1,0:T(1,128)S(1)} all-to-all(f32[1152,1,256]{2,1,0:T(1,128)S(1)} %copy.15), channel_id=1, replica_groups=mesh['ens'=2,'comp'=4,'lat'=2,'lon'=2] {'comp'}, dimensions={0} | all-to-all | bytes 2359296 | tf_op jit(solution)/shard_map/all_to_all | solution.py:170
  195.1 0.8 copy.16
  195.9 1.5 reshape.71
  (71 shorter events, 5.2 us)
Async XLA Ops:
  0.0 8.6 %copy-start = (f32[16,32]{1,0:T(8,128)S(1)}, f32[16,32]{1,0:T(8,128)}, u32[]{:S(2)}) copy-start(f32[16,32]{1,0:T(8,128)} %param.13) | copy-start | bytes 6148
  0.7 8.2 %collective-permute-start.4 = (s32[3,8,128]{2,1,0:T(8,128)S(1)}, s32[3,8,128]{2,1,0:T(8,128)S(1)}, u32[]{:S(2)}, u32[]{:S(2)}) collective-permute-start(s32[3,8,128]{2,1,0:T(8,128)S(1)} %pad_add_fusion.2), channel_id=1, source_target_pairs={{0,2},{2,0},{1,3},{3,1},{4,6},{6,4},{5,7},{7,5},{8,10},{10,8},{9,1... | collective-permute-start | bytes 36872 | tf_op jit(solution)/shard_map/ppermute | solution.py:23
  3.7 5.3 %collective-permute-start.5 = (s32[3,8,128]{2,1,0:T(8,128)S(1)}, s32[3,8,128]{2,1,0:T(8,128)S(1)}, u32[]{:S(2)}, u32[]{:S(2)}) collective-permute-start(s32[3,8,128]{2,1,0:T(8,128)S(1)} %pad_add_fusion.2), channel_id=1, source_target_pairs={{2,0},{0,2},{3,1},{1,3},{6,4},{4,6},{7,5},{5,7},{10,8},{8,10},{11,... | collective-permute-start | bytes 36872 | tf_op jit(solution)/shard_map/ppermute | solution.py:26
  6.2 2.8 %copy-start.2 = (s32[8,128]{1,0:T(8,128)S(1)}, s32[8,128]{1,0:T(8,128)}, u32[]{:S(2)}) copy-start(s32[8,128]{1,0:T(8,128)} %param.10) | copy-start | bytes 12292
  6.2 2.8 %copy-start.3 = (s32[8,128]{1,0:T(8,128)S(1)}, s32[8,128]{1,0:T(8,128)}, u32[]{:S(2)}) copy-start(s32[8,128]{1,0:T(8,128)} %param.12) | copy-start | bytes 12292
  6.2 2.8 %copy-start.4 = (s32[8,128]{1,0:T(8,128)S(1)}, s32[8,128]{1,0:T(8,128)}, u32[]{:S(2)}) copy-start(s32[8,128]{1,0:T(8,128)} %param.11) | copy-start | bytes 12292
  6.4 4.2 %copy-start.8 = (f32[16,2]{0,1:T(2,128)S(1)}, f32[16,2]{0,1:T(2,128)}, u32[]{:S(2)}) copy-start(f32[16,2]{0,1:T(2,128)} %param.14) | copy-start | bytes 388
  6.5 12.1 %collective-permute-start = (f32[288,2,128]{0,2,1:T(8,128)S(1)}, f32[288,2,128]{0,2,1:T(8,128)S(1)}, u32[]{:S(2)}, u32[]{:S(2)}) collective-permute-start(f32[288,2,128]{0,2,1:T(8,128)S(1)} %get-tuple-element.41), channel_id=1, source_target_pairs={{0,2},{2,0},{1,3},{3,1},{4,6},{6,4},{5,7},{7,5},{8,10},{10,8},{9,1... | collective-permute-start | bytes 884744 | tf_op jit(solution)/shard_map/ppermute | solution.py:23
  8.6 17.0 %collective-permute-start.1 = (f32[288,2,128]{0,2,1:T(8,128)S(1)}, f32[288,2,128]{0,2,1:T(8,128)S(1)}, u32[]{:S(2)}, u32[]{:S(2)}) collective-permute-start(f32[288,2,128]{0,2,1:T(8,128)S(1)} %get-tuple-element.42), channel_id=1, source_target_pairs={{2,0},{0,2},{3,1},{1,3},{6,4},{4,6},{7,5},{5,7},{10,8},{8,10},{11,... | collective-permute-start | bytes 884744 | tf_op jit(solution)/shard_map/ppermute | solution.py:26
  9.1 1.2 collective-permute-start.6
  9.1 1.4 collective-permute-start.7
  25.6 1.3 collective-permute-start.2
  25.7 1.4 collective-permute-start.3
  32.1 12.1 %collective-permute-start.8 = (f32[288,2,128]{0,2,1:T(8,128)S(1)}, f32[288,2,128]{0,2,1:T(8,128)S(1)}, u32[]{:S(2)}, u32[]{:S(2)}) collective-permute-start(f32[288,2,128]{0,2,1:T(8,128)S(1)} %get-tuple-element.39), channel_id=1, source_target_pairs={{0,2},{2,0},{1,3},{3,1},{4,6},{6,4},{5,7},{7,5},{8,10},{10,8},{9,1... | collective-permute-start | bytes 884744 | tf_op jit(solution)/shard_map/ppermute | solution.py:23
  33.9 18.1 %collective-permute-start.9 = (f32[288,2,128]{0,2,1:T(8,128)S(1)}, f32[288,2,128]{0,2,1:T(8,128)S(1)}, u32[]{:S(2)}, u32[]{:S(2)}) collective-permute-start(f32[288,2,128]{0,2,1:T(8,128)S(1)} %get-tuple-element.40), channel_id=1, source_target_pairs={{2,0},{0,2},{3,1},{1,3},{6,4},{4,6},{7,5},{5,7},{10,8},{8,10},{11,... | collective-permute-start | bytes 884744 | tf_op jit(solution)/shard_map/ppermute | solution.py:26
  52.0 1.3 collective-permute-start.10
  52.0 1.4 collective-permute-start.11
  57.3 12.1 %collective-permute-start.12 = (f32[288,2,128]{0,2,1:T(8,128)S(1)}, f32[288,2,128]{0,2,1:T(8,128)S(1)}, u32[]{:S(2)}, u32[]{:S(2)}) collective-permute-start(f32[288,2,128]{0,2,1:T(8,128)S(1)} %get-tuple-element.37), channel_id=1, source_target_pairs={{0,2},{2,0},{1,3},{3,1},{4,6},{6,4},{5,7},{7,5},{8,10},{10,8},{9,1... | collective-permute-start | bytes 884744 | tf_op jit(solution)/shard_map/ppermute | solution.py:23
  59.1 18.1 %collective-permute-start.13 = (f32[288,2,128]{0,2,1:T(8,128)S(1)}, f32[288,2,128]{0,2,1:T(8,128)S(1)}, u32[]{:S(2)}, u32[]{:S(2)}) collective-permute-start(f32[288,2,128]{0,2,1:T(8,128)S(1)} %get-tuple-element.38), channel_id=1, source_target_pairs={{2,0},{0,2},{3,1},{1,3},{6,4},{4,6},{7,5},{5,7},{10,8},{8,10},{11,... | collective-permute-start | bytes 884744 | tf_op jit(solution)/shard_map/ppermute | solution.py:26
  77.2 1.3 collective-permute-start.14
  77.3 1.4 collective-permute-start.15
  82.5 12.1 %collective-permute-start.16 = (f32[288,2,128]{0,2,1:T(8,128)S(1)}, f32[288,2,128]{0,2,1:T(8,128)S(1)}, u32[]{:S(2)}, u32[]{:S(2)}) collective-permute-start(f32[288,2,128]{0,2,1:T(8,128)S(1)} %get-tuple-element.35), channel_id=1, source_target_pairs={{0,2},{2,0},{1,3},{3,1},{4,6},{6,4},{5,7},{7,5},{8,10},{10,8},{9,1... | collective-permute-start | bytes 884744 | tf_op jit(solution)/shard_map/ppermute | solution.py:23
  84.3 18.1 %collective-permute-start.17 = (f32[288,2,128]{0,2,1:T(8,128)S(1)}, f32[288,2,128]{0,2,1:T(8,128)S(1)}, u32[]{:S(2)}, u32[]{:S(2)}) collective-permute-start(f32[288,2,128]{0,2,1:T(8,128)S(1)} %get-tuple-element.36), channel_id=1, source_target_pairs={{2,0},{0,2},{3,1},{1,3},{6,4},{4,6},{7,5},{5,7},{10,8},{8,10},{11,... | collective-permute-start | bytes 884744 | tf_op jit(solution)/shard_map/ppermute | solution.py:26
  102.4 1.3 collective-permute-start.18
  102.5 1.4 collective-permute-start.19
  109.4 5.2 %copy-start.5 = (f32[2,1152,4]{1,2,0:T(4,128)S(1)}, f32[2,1152,4]{1,2,0:T(4,128)}, u32[]{:S(2)}) copy-start(f32[2,1152,4]{1,2,0:T(4,128)} %param.17) | copy-start | bytes 110596
  109.4 5.4 %copy-start.6 = (s32[2,1152,4]{1,2,0:T(4,128)S(1)}, s32[2,1152,4]{1,2,0:T(4,128)}, u32[]{:S(2)}) copy-start(s32[2,1152,4]{1,2,0:T(4,128)} %param.16) | copy-start | bytes 110596
  109.4 34.3 %all-to-all-start = ((f32[288,4,256]{2,0,1:T(8,128)}), f32[288,4,256]{2,0,1:T(8,128)S(1)}, u32[]{:S(2)}, u32[]{:S(2)}) async-start(f32[288,4,256]{2,0,1:T(8,128)} %copy.14), calls=%async_computation | async-start | bytes 2359296 | tf_op jit(solution)/shard_map/all_to_all | solution.py:167
  143.7 4.4 %copy-start.7 = (f32[1152]{0:T(1024)S(1)}, f32[1152]{0:T(1024)}, u32[]{:S(2)}) copy-start(f32[1152]{0:T(1024)} %param.15) | copy-start | bytes 13828
  195.1 2.3 %copy-start.1 = (f32[16,32]{1,0:T(8,128)S(1)}, f32[16,32]{1,0:T(8,128)}, u32[]{:S(2)}) copy-start(f32[16,32]{1,0:T(8,128)} %param.13) | copy-start | bytes 6148
where the time goes:
time: 198 us; the launch traced here: 197 us
  waiting for transfers between devices  97.5 us (49%)
  blocking collectives  30.6 us (15%)
  matrix products  19.6 us (10%)
  starting transfers between devices  19.4 us (10%)
  other arithmetic  18.7 us (9%)
  local copies, waits for them, and re-layouts  11 us (6%)
    ppermute x10, waiting for transfers between devices, with_halo(): lax.ppermute(lax.slice_in_dim(block, block.shape[dim] - width, None, axis...  37.4 us
    ppermute x10, waiting for transfers between devices, with_halo(): lax.ppermute(lax.slice_in_dim(block, 0, width, axis=dim), axis, backward)  31.2 us
    all_to_all x1, blocking collectives, local(): lax.all_to_all(arrived, 'comp', split_axis=0, concat_axis=1, tiled=True)  30.6 us
    all_to_all x1, waiting for transfers between devices, local(): lax.all_to_all(outgoing, 'comp', split_axis=1, concat_axis=0, tiled=True)  28.8 us
    ppermute x10, starting transfers between devices, with_halo(): lax.ppermute(lax.slice_in_dim(block, block.shape[dim] - width, None, axis...  10.7 us
    add x8, other arithmetic, face_flux(): jnp.maximum(face_speed, 0.0) * upwind_left  8.76 us
    all_to_all x1, starting transfers between devices, local(): lax.all_to_all(outgoing, 'comp', split_axis=1, concat_axis=0, tiled=True)  5.24 us
    reshape x1, local copies, waits for them, and re-layouts, local(): interact(point_grid, kernel_plus, kernel_minus, coupling)  4.89 us
  transfers between devices with their start and end apart: 21, of which 19 were waited for; matrix products, arithmetic and copies ran while one was open for 4% of the time, Pallas kernels for 0%

commit v1 on v0

--- a/solution.py
+++ b/solution.py
@@ -1,8 +1,12 @@
+import functools
 import math
 
 import jax
 import jax.numpy as jnp
+import numpy as np
 from jax import lax
+from jax.experimental import pallas as pl
+from jax.experimental.pallas import tpu as pltpu
 from jax.sharding import PartitionSpec as P
 
 NDIR = 36
@@ -171,6 +175,430 @@
     return returned.reshape(comps_local, lat_rows, lon_cols)
 
 
+CHUNK = 24
+BLOCK = 4
+TILE = 128
+MESH = pl.DeviceIdType.MESH
+
+
+def limited(upper, lower):
+    return jnp.maximum(
+        jnp.minimum(upper, lower), jnp.minimum(jnp.maximum(upper, lower), 0.0)
+    )
+
+
+def aligned(index, unit):
+    return pl.multiple_of(index, unit)
+
+
+def step_kernel(
+    nz,
+    nx,
+    nc,
+    spec,
+    grids,
+    coupling,
+    qi_cols,
+    qw_cols,
+    qi_rows,
+    qw_rows,
+    speed_table,
+    current_table,
+    turns,
+    out,
+    gbuf,
+    buf,
+    fields,
+    base,
+    send,
+    arrived,
+    low,
+    kern,
+    kern_t,
+    source,
+    source_low,
+    result,
+    returned,
+    sem_grid_s,
+    sem_grid_r,
+    sem_a_s,
+    sem_a_r,
+    sem_c_s,
+    sem_c_r,
+    sem_d_s,
+    sem_d_r,
+):
+    z, x, c = lax.axis_index("comp"), lax.axis_index("lat"), lax.axis_index("lon")
+    group = nx * nc
+    me = x * nc + c
+    rows, cols = returned.shape[0], returned.shape[2]
+    comps_local = returned.shape[1]
+    comps_own = buf.shape[1] // rows
+    comp_total = arrived.shape[1]
+    row_share = rows // nz
+    chunks = comps_own // CHUNK
+    all_rows, all_cols = rows * nx, cols * nc
+
+    def place(dz, dg):
+        other = lax.rem(me + dg, group)
+        return lax.rem(z + dz, nz), other, {
+            "comp": lax.rem(z + dz, nz),
+            "lat": other // nc,
+            "lon": lax.rem(other, nc),
+        }
+
+    barrier = pltpu.get_barrier_semaphore()
+    for dz in range(nz):
+        for dg in range(group):
+            if dz or dg:
+                _, _, there = place(dz, dg)
+                pl.semaphore_signal(barrier, inc=1, device_id=there, device_id_type=MESH)
+    pl.semaphore_wait(barrier, nz * group - 1)
+
+    pltpu.make_async_copy(grids, gbuf.at[me], sem_grid_r.at[me]).start()
+    for dg in range(1, group):
+        _, other, there = place(0, dg)
+        pltpu.make_async_remote_copy(
+            src_ref=grids,
+            dst_ref=gbuf.at[me],
+            send_sem=sem_grid_s.at[dg],
+            recv_sem=sem_grid_r.at[me],
+            device_id=there,
+            device_id_type=MESH,
+        ).start()
+    span = CHUNK * rows
+
+    @pl.loop(0, chunks)
+    def _(ch):
+        here = pl.ds(aligned(ch * span, span), span)
+        for dg in range(group):
+            _, other, there = place(0, dg)
+            taken = pl.ds(aligned(other * (comps_own * rows) + ch * span, span), span)
+            if dg == 0:
+                pltpu.make_async_copy(
+                    spec.at[taken], buf.at[me, here], sem_a_r.at[me, ch]
+                ).start()
+            else:
+                pltpu.make_async_remote_copy(
+                    src_ref=spec.at[taken],
+                    dst_ref=buf.at[me, here],
+                    send_sem=sem_a_s.at[dg, ch],
+                    recv_sem=sem_a_r.at[me, ch],
+                    device_id=there,
+                    device_id_type=MESH,
+                ).start()
+
+    lanes = lax.broadcasted_iota(jnp.int32, (TILE, comp_total), 1)
+    subs = lax.broadcasted_iota(jnp.int32, (TILE, comp_total), 0)
+
+    def make_dense(t):
+        start = aligned(t * TILE, TILE)
+        spot = pl.ds(start, TILE)
+        for side in range(2):
+            block = jnp.zeros((TILE, comp_total), jnp.float32)
+            for corner in range(4):
+                col = side * 4 + corner
+                block = jnp.where(
+                    lanes == qi_cols[spot, col : col + 1], qw_cols[spot, col : col + 1], block
+                )
+            kern[side, spot, :] = block.astype(jnp.bfloat16)
+
+    def make_dense_t(t):
+        start = aligned(t * TILE, TILE)
+        spot = pl.ds(start, TILE)
+        both = []
+        for side in range(2):
+            block = jnp.zeros((TILE, comp_total), jnp.float32)
+            for corner in range(4):
+                row = side * 4 + corner
+                block = jnp.where(
+                    subs + start == qi_rows[row : row + 1, :], qw_rows[row : row + 1, :], block
+                )
+            both.append(block)
+        kern_t[spot, :] = (both[0] + both[1]).astype(jnp.bfloat16)
+
+    for g in range(group):
+        pltpu.make_async_copy(gbuf.at[g], gbuf.at[g], sem_grid_r.at[g]).wait()
+
+    def whole(pick):
+        return jnp.concatenate(
+            [
+                jnp.concatenate([pick(i * nc + j) for j in range(nc)], axis=1)
+                for i in range(nx)
+            ],
+            axis=0,
+        )
+
+    row_ids = lax.broadcasted_iota(jnp.int32, (all_rows, all_cols), 0)
+
+    def east(v):
+        return pltpu.roll(v, all_cols - 1, 1)
+
+    def west(v):
+        return pltpu.roll(v, 1, 1)
+
+    def north(v):
+        return jnp.where(row_ids < all_rows - 1, pltpu.roll(v, all_rows - 1, 0), 0.0)
+
+    def south(v):
+        return jnp.where(row_ids > 0, pltpu.roll(v, 1, 0), 0.0)
+
+    wet = whole(lambda g: gbuf[g, 0]).astype(jnp.float32)
+    depth = whole(lambda g: gbuf[g, 1])
+    current = whole(lambda g: gbuf[g, 2])
+    wet_x = 0.5 * (wet * east(wet))
+    wet_y = 0.5 * (wet * north(wet))
+    flow_x = jnp.zeros_like(wet)
+    flow_y = jnp.zeros_like(wet)
+    for n in range(current_table.shape[0]):
+        flow_x = jnp.where(current == n, current_table[n, 0], flow_x)
+        flow_y = jnp.where(current == n, current_table[n, 1], flow_y)
+    base[0] = (flow_x + east(flow_x)) * wet_x
+    base[1] = (flow_y + north(flow_y)) * wet_y
+    base[2] = wet
+    first_freq = (z * comps_local + me * comps_own) // NDIR
+    for j in range(comps_own // NDIR):
+        speed = jnp.zeros_like(wet)
+        for n in range(speed_table.shape[0]):
+            speed = jnp.where(depth == n, speed_table[n, first_freq + j], speed)
+        fields[j, 0] = (speed + east(speed)) * wet_x
+        fields[j, 1] = (speed + north(speed)) * wet_y
+
+    def propagate(first):
+        freq = first // NDIR
+        angle = lax.rem(first, NDIR)
+        for k in range(BLOCK):
+            spot = pl.ds(aligned((first + k) * rows, rows), rows)
+            energy = whole(lambda g: buf[g, spot, :]) * base[2]
+            speed_x = fields[freq, 0] * turns[0, angle + k] + base[0]
+            speed_y = fields[freq, 1] * turns[1, angle + k] + base[1]
+            size_x, size_y = jnp.abs(speed_x), jnp.abs(speed_y)
+            half_x = 0.5 * size_x * (1.0 - size_x)
+            half_y = 0.5 * size_y * (1.0 - size_y)
+            for _ in range(SUBSTEPS):
+                ahead, behind = east(energy), west(energy)
+                slope = limited(ahead - energy, energy - behind)
+                flux_x = speed_x * jnp.where(speed_x > 0.0, energy, ahead) + half_x * jnp.where(
+                    speed_x > 0.0, slope, east(slope)
+                )
+                ahead, behind = north(energy), south(energy)
+                slope = limited(ahead - energy, energy - behind)
+                flux_y = speed_y * jnp.where(speed_y > 0.0, energy, ahead) + half_y * jnp.where(
+                    speed_y > 0.0, slope, pltpu.roll(slope, all_rows - 1, 0)
+                )
+                energy = (
+                    energy - (flux_x - west(flux_x)) - (flux_y - pltpu.roll(flux_y, 1, 0))
+                )
+            for i in range(nx):
+                for j in range(nc):
+                    buf[i * nc + j, spot, :] = energy[
+                        i * rows : (i + 1) * rows, j * cols : (j + 1) * cols
+                    ]
+
+    own_first = (z * group + me) * comps_own
+
+    def pass_on(row, start, count, sem_row):
+        there_spot = pl.ds(aligned(own_first + start, 8), count)
+        here_spot = pl.ds(aligned(start, 8), count)
+        for dz in (2, 1, 3, 0) if nz == 4 else range(nz):
+            for dg in range(group):
+                to_z, other, there = place(dz, dg)
+                piece = send.at[other, to_z * row_share + row, here_spot]
+                target = arrived.at[row, there_spot]
+                if dz or dg:
+                    pltpu.make_async_remote_copy(
+                        src_ref=piece,
+                        dst_ref=target,
+                        send_sem=sem_c_s.at[row],
+                        recv_sem=sem_c_r.at[row],
+                        device_id=there,
+                        device_id_type=MESH,
+                    ).start()
+                else:
+                    pltpu.make_async_copy(piece, target, sem_c_r.at[row]).start()
+
+    @pl.loop(0, chunks)
+    def _(ch):
+        here = pl.ds(aligned(ch * span, span), span)
+        for g in range(group):
+            pltpu.make_async_copy(
+                buf.at[g, here], buf.at[g, here], sem_a_r.at[g, ch]
+            ).wait()
+
+        @pl.loop(0, CHUNK // BLOCK)
+        def _(b):
+            propagate(ch * CHUNK + b * BLOCK)
+
+        for g in range(group):
+            for row in range(rows):
+                send[g, row, pl.ds(aligned(ch * CHUNK, 8), CHUNK), :] = buf[
+                    g, pl.ds(ch * span + row, CHUNK, stride=rows), :
+                ]
+        pass_on(0, ch * CHUNK, CHUNK, 0)
+
+    for row in range(1, row_share):
+        pass_on(row, 0, comps_own, row)
+
+    pl.loop(0, comp_total // TILE)(make_dense)
+    pl.loop(0, comp_total // TILE)(make_dense_t)
+
+    for row in range(row_share):
+        pltpu.make_async_copy(arrived.at[row], arrived.at[row], sem_c_r.at[row]).wait()
+        low[...] = arrived[row].astype(jnp.bfloat16)
+
+        @pl.loop(0, comp_total // TILE)
+        def _(t):
+            spot = pl.ds(aligned(t * TILE, TILE), TILE)
+            plus = jnp.dot(kern[0, spot, :], low[...], preferred_element_type=jnp.float32)
+            minus = jnp.dot(kern[1, spot, :], low[...], preferred_element_type=jnp.float32)
+            energy = arrived[row, spot, :]
+            gain = coupling[spot, :] * (
+                energy * energy * (plus_factor * plus + minus_factor * minus)
+                - cross_factor * energy * plus * minus
+            )
+            source[spot, :] = gain
+            source_low[spot, :] = gain.astype(jnp.bfloat16)
+
+        for dz in (2, 1, 3, 0) if nz == 4 else range(nz):
+            to_z, _, there = place(dz, 0)
+            first = to_z * comps_local
+
+            @pl.loop(0, comps_local // 96)
+            def _(t):
+                spot = pl.ds(aligned(first + t * 96, 32), 96)
+                net = (
+                    jnp.dot(kern_t[spot, :], source_low[...], preferred_element_type=jnp.float32)
+                    - 2.0 * source[spot, :]
+                )
+                result[row, spot, :] = arrived[row, spot, :] + net / (1.0 + jnp.abs(net))
+
+            piece = result.at[row, pl.ds(aligned(first, 8), comps_local)]
+            target = returned.at[z * row_share + row]
+            if dz:
+                pltpu.make_async_remote_copy(
+                    src_ref=piece,
+                    dst_ref=target,
+                    send_sem=sem_d_s.at[row],
+                    recv_sem=sem_d_r.at[row],
+                    device_id=there,
+                    device_id_type=MESH,
+                ).start()
+            else:
+                pltpu.make_async_copy(piece, target, sem_d_r.at[row]).start()
+
+    for row in range(row_share):
+        all_z = returned.at[pl.ds(0, nz)]
+        pltpu.make_async_copy(all_z, all_z, sem_d_r.at[row]).wait()
+        for quarter in range(nz):
+            line = quarter * row_share + row
+            out[pl.ds(line, comps_local, stride=rows), :] = returned[line]
+
+    for dg in range(1, group):
+        pltpu.make_async_copy(grids, gbuf.at[0], sem_grid_s.at[dg]).wait()
+
+        @pl.loop(0, chunks)
+        def _(ch):
+            here = pl.ds(0, span)
+            pltpu.make_async_copy(buf.at[0, here], buf.at[0, here], sem_a_s.at[dg, ch]).wait()
+
+    for row in range(row_share):
+        sent = arrived.at[row, pl.ds(0, comp_total - comps_own)]
+        pltpu.make_async_copy(sent, sent, sem_c_s.at[row]).wait()
+        sent = returned.at[pl.ds(0, nz - 1)]
+        pltpu.make_async_copy(sent, sent, sem_d_s.at[row]).wait()
+
+
+def fused(nz, nx, nc, *arrays):
+    (
+        spectrum,
+        sea_mask,
+        depth_class,
+        current_class,
+        speed_table,
+        current_table,
+        coupling,
+        quad_index,
+        quad_weight,
+    ) = arrays
+    comps_local, rows, cols = spectrum.shape
+    comp_total = coupling.shape[0]
+    group = nx * nc
+    own = comps_local // group
+    share = rows // nz
+    turn = 2.0 * math.pi / NDIR * np.arange(NDIR)
+    turns = jnp.asarray(np.stack([np.cos(turn), np.sin(turn)]), jnp.float32)
+    vmem = pl.BlockSpec(memory_space=pltpu.VMEM)
+    smem = pl.BlockSpec(memory_space=pltpu.SMEM)
+    f32, bf16, i32 = jnp.float32, jnp.bfloat16, jnp.int32
+    dma = pltpu.SemaphoreType.DMA
+    qi_rows = quad_index.transpose(0, 2, 1).reshape(8, comp_total)
+    qw_rows = quad_weight.transpose(0, 2, 1).reshape(8, comp_total)
+    out = pl.pallas_call(
+        functools.partial(step_kernel, nz, nx, nc),
+        name="wave_step",
+        out_shape=jax.ShapeDtypeStruct((comps_local * rows, cols), f32),
+        in_specs=[pl.BlockSpec(memory_space=pl.ANY)] + [vmem] * 6 + [smem] * 3,
+        out_specs=vmem,
+        scratch_shapes=[
+            pltpu.VMEM((group, 3, rows, cols), i32),
+            pltpu.VMEM((group, own * rows, cols), f32),
+            pltpu.VMEM((own // NDIR, 2, rows * nx, cols * nc), f32),
+            pltpu.VMEM((3, rows * nx, cols * nc), f32),
+            pltpu.VMEM((group, rows, own, cols), f32),
+            pltpu.VMEM((share, comp_total, cols), f32),
+            pltpu.VMEM((comp_total, cols), bf16),
+            pltpu.VMEM((2, comp_total, comp_total), bf16),
+            pltpu.VMEM((comp_total, comp_total), bf16),
+            pltpu.VMEM((comp_total, cols), f32),
+            pltpu.VMEM((comp_total, cols), bf16),
+            pltpu.VMEM((share, comp_total, cols), f32),
+            pltpu.VMEM((rows, comps_local, cols), f32),
+            dma((group,)),
+            dma((group,)),
+            dma((group, own // CHUNK)),
+            dma((group, own // CHUNK)),
+            dma((share,)),
+            dma((share,)),
+            dma((share,)),
+            dma((share,)),
+        ],
+        compiler_params=pltpu.CompilerParams(
+            collective_id=0, has_side_effects=True, vmem_limit_bytes=60 * 1024 * 1024
+        ),
+    )(
+        spectrum.reshape(comps_local * rows, cols),
+        jnp.stack([sea_mask, depth_class, current_class]),
+        coupling[:, None],
+        qi_rows.T,
+        qw_rows.T,
+        qi_rows,
+        qw_rows,
+        speed_table,
+        current_table,
+        turns,
+    )
+    return out.reshape(comps_local, rows, cols)
+
+
+def step(*arrays):
+    comps_local, rows, cols = arrays[0].shape
+    comp_total = arrays[6].shape[0]
+    nz, nx, nc = (lax.axis_size(a) for a in ("comp", "lat", "lon"))
+    own = comps_local // (nx * nc)
+    fits = (
+        comps_local % (nx * nc) == 0
+        and own % NDIR == 0
+        and own % CHUNK == 0
+        and NDIR % BLOCK == 0
+        and rows == 8
+        and cols % 128 == 0
+        and rows % nz == 0
+        and comp_total % TILE == 0
+        and comps_local % 96 == 0
+    )
+    return fused(nz, nx, nc, *arrays) if fits else local(*arrays)
+
+
 def solution(mesh):
     placed = (
         P(("ens", "comp"), "lat", "lon"),
@@ -184,7 +612,7 @@
         P(),
     )
     return jax.shard_map(
-        local,
+        step,
         mesh=mesh,
         in_specs=placed,
         out_specs=P(("ens", "comp"), "lat", "lon"),

time: 198 us -> 83 us (0.42)
  the two profiles are of different devices: /device:TPU:0 before, /device:TPU:19 now
where the time goes in v1:
time: 83 us; the launch traced here: 82.5 us
  Pallas kernels  72.7 us (88%)
  local copies, waits for them, and re-layouts  8.52 us (10%)
  other arithmetic  1.31 us (2%)
    pallas_call x1, Pallas kernels, fused(): pl.pallas_call(functools.partial(step_kernel, nz, nx, nc), name='wave_ste...  72.7 us
    unnamed x8, local copies, waits for them, and re-layouts  3.72 us
    transpose x2, local copies, waits for them, and re-layouts, fused(): out = pl.pallas_call(functools.partial(step_kernel, nz, nx, nc), name='wa...  2.19 us

profile of v1, /device:TPU:19, one launch (start us, length us, event | category | flops | bytes accessed | tf_op | source)
XLA Modules:
  0.0 82.5 jit_solution(1271027145355030378)
XLA Ops:
  0.0 0.0 copy-start.2
  0.0 1.3 %copy.17.current_table = f32[16,2]{1,0:T(8,128)} copy(f32[16,2]{0,1:T(2,128)} %param.15) | data formatting | bytes 256 | tf_op args[5]
  1.3 1.3 %pad_add_fusion.grids = s32[3,8,128]{2,1,0:T(8,128)} fusion(s32[1,8,128]{2,1,0:T(8,128)} %bitcast.15, s32[1,8,128]{2,1,0:T(8,128)} %bitcast.16, s32[1,8,128]{2,1,0:T(8,128)} %bitcast.17), kind=kLoop, calls=%fused_computation | loop fusion | flops 6144 | bytes 24576 | tf_op jit(solution)/shard_map/stack | solution.py:570
  2.7 0.8 reshape.13.qi_rows
  3.4 0.0 copy-start
  3.5 0.8 reshape.14.qw_rows
  4.3 0.0 copy-start.1
  4.3 1.1 %copy.16.qw_cols = f32[1152,8]{1,0:T(8,128)} copy(f32[1152,8]{0,1:T(8,128)S(1)} %bitcast.12) | data formatting | bytes 73728 | tf_op jit(solution)/shard_map/transpose | solution.py:573
  5.3 1.1 %copy.15.qi_cols = s32[1152,8]{1,0:T(8,128)} copy(s32[1152,8]{0,1:T(8,128)S(1)} %bitcast.11) | data formatting | bytes 73728 | tf_op jit(solution)/shard_map/transpose | solution.py:572
  6.5 0.0 copy-done.2
  6.5 1.0 %broadcast_in_dim.4.coupling = f32[1152,1]{1,0:T(8,128)} reshape(f32[1152]{0:T(1024)S(1)} %copy-done.2) | data formatting | bytes 9216 | tf_op jit(solution)/shard_map/broadcast_in_dim | solution.py:571
  7.5 0.0 copy-done
  7.5 0.0 copy-done.1
  7.5 72.7 %wave_step.1 = f32[2304,128]{1,0:T(8,128)} custom-call(f32[2304,128]{1,0:T(8,128)} %bitcast.10, s32[3,8,128]{2,1,0:T(8,128)} %pad_add_fusion.grids, f32[1152,1]{1,0:T(8,128)} %broadcast_in_dim.4.coupling, s32[1152,8]{1,0:T(8,128)} %copy.15.qi_cols, f32[1152,8]{1,0:T(8,128)} %copy.16.qw_cols, s32[8,1152]{1,0:T(8,128)} %copy-done, f32[8,1152]{1,0:T(8,128)} %copy-done.1, ...), custom_call_target="tpu_custom_call" | custom-call | tf_op jit(solution)/shard_map/wave_step/pallas_call | solution.py:536
  80.2 2.4 %copy.19 = f32[288,8,128]{2,1,0:T(8,128)} copy(f32[288,8,128]{2,1,0:T(8,128)} %bitcast.9) | data formatting | bytes 2359296
Async XLA Ops:
  0.0 6.5 %copy-start.2 = (f32[1152]{0:T(1024)S(1)}, f32[1152]{0:T(1024)}, u32[]{:S(2)}) copy-start(f32[1152]{0:T(1024)} %param.16) | copy-start | bytes 13828
  3.4 4.0 %copy-start = (s32[8,1152]{1,0:T(8,128)}, s32[8,1152]{1,0:T(8,128)S(1)}, u32[]{:S(2)}) copy-start(s32[8,1152]{1,0:T(8,128)S(1)} %reshape.13.qi_rows) | copy-start | bytes 110596
  4.3 3.2 %copy-start.1 = (f32[8,1152]{1,0:T(8,128)}, f32[8,1152]{1,0:T(8,128)S(1)}, u32[]{:S(2)}) copy-start(f32[8,1152]{1,0:T(8,128)S(1)} %reshape.14.qw_rows) | copy-start | bytes 110596

commit v2 on v1

--- a/solution.py
+++ b/solution.py
@@ -176,7 +176,7 @@
 
 
 CHUNK = 24
-BLOCK = 4
+BLOCK = 12
 TILE = 128
 MESH = pl.DeviceIdType.MESH
 
@@ -196,12 +196,12 @@
     nx,
     nc,
     spec,
-    grids,
+    sea_mask,
+    depth_class,
+    current_class,
     coupling,
-    qi_cols,
-    qw_cols,
-    qi_rows,
-    qw_rows,
+    quad_index,
+    quad_weight,
     speed_table,
     current_table,
     turns,
@@ -215,6 +215,7 @@
     low,
     kern,
     kern_t,
+    strength,
     source,
     source_low,
     result,
@@ -255,17 +256,18 @@
                 pl.semaphore_signal(barrier, inc=1, device_id=there, device_id_type=MESH)
     pl.semaphore_wait(barrier, nz * group - 1)
 
-    pltpu.make_async_copy(grids, gbuf.at[me], sem_grid_r.at[me]).start()
-    for dg in range(1, group):
-        _, other, there = place(0, dg)
-        pltpu.make_async_remote_copy(
-            src_ref=grids,
-            dst_ref=gbuf.at[me],
-            send_sem=sem_grid_s.at[dg],
-            recv_sem=sem_grid_r.at[me],
-            device_id=there,
-            device_id_type=MESH,
-        ).start()
+    for i, grid in enumerate((sea_mask, depth_class, current_class)):
+        pltpu.make_async_copy(grid, gbuf.at[me, i], sem_grid_r.at[me, i]).start()
+        for dg in range(1, group):
+            _, other, there = place(0, dg)
+            pltpu.make_async_remote_copy(
+                src_ref=grid,
+                dst_ref=gbuf.at[me, i],
+                send_sem=sem_grid_s.at[dg, i],
+                recv_sem=sem_grid_r.at[me, i],
+                device_id=there,
+                device_id_type=MESH,
+            ).start()
     span = CHUNK * rows
 
     @pl.loop(0, chunks)
@@ -294,12 +296,20 @@
     def make_dense(t):
         start = aligned(t * TILE, TILE)
         spot = pl.ds(start, TILE)
+        strength[spot, :] = jnp.broadcast_to(coupling[pl.ds(t, 1), :], (cols, TILE)).T
+        indices, weights = (
+            jnp.concatenate(
+                [table[side, :, spot].astype(jnp.float32) for side in range(2)], axis=0
+            ).T
+            for table in (quad_index, quad_weight)
+        )
+        indices = indices.astype(jnp.int32)
         for side in range(2):
             block = jnp.zeros((TILE, comp_total), jnp.float32)
             for corner in range(4):
                 col = side * 4 + corner
                 block = jnp.where(
-                    lanes == qi_cols[spot, col : col + 1], qw_cols[spot, col : col + 1], block
+                    lanes == indices[:, col : col + 1], weights[:, col : col + 1], block
                 )
             kern[side, spot, :] = block.astype(jnp.bfloat16)
 
@@ -310,15 +320,16 @@
         for side in range(2):
             block = jnp.zeros((TILE, comp_total), jnp.float32)
             for corner in range(4):
-                row = side * 4 + corner
+                one = slice(corner, corner + 1)
                 block = jnp.where(
-                    subs + start == qi_rows[row : row + 1, :], qw_rows[row : row + 1, :], block
+                    subs + start == quad_index[side, one, :], quad_weight[side, one, :], block
                 )
             both.append(block)
         kern_t[spot, :] = (both[0] + both[1]).astype(jnp.bfloat16)
 
     for g in range(group):
-        pltpu.make_async_copy(gbuf.at[g], gbuf.at[g], sem_grid_r.at[g]).wait()
+        for i in range(3):
+            pltpu.make_async_copy(gbuf.at[g, i], gbuf.at[g, i], sem_grid_r.at[g, i]).wait()
 
     def whole(pick):
         return jnp.concatenate(
@@ -350,9 +361,9 @@
     wet_y = 0.5 * (wet * north(wet))
     flow_x = jnp.zeros_like(wet)
     flow_y = jnp.zeros_like(wet)
-    for n in range(current_table.shape[0]):
-        flow_x = jnp.where(current == n, current_table[n, 0], flow_x)
-        flow_y = jnp.where(current == n, current_table[n, 1], flow_y)
+    for n in range(current_table.shape[1]):
+        flow_x = jnp.where(current == n, current_table[0, n], flow_x)
+        flow_y = jnp.where(current == n, current_table[1, n], flow_y)
     base[0] = (flow_x + east(flow_x)) * wet_x
     base[1] = (flow_y + north(flow_y)) * wet_y
     base[2] = wet
@@ -452,7 +463,7 @@
             plus = jnp.dot(kern[0, spot, :], low[...], preferred_element_type=jnp.float32)
             minus = jnp.dot(kern[1, spot, :], low[...], preferred_element_type=jnp.float32)
             energy = arrived[row, spot, :]
-            gain = coupling[spot, :] * (
+            gain = strength[spot, :] * (
                 energy * energy * (plus_factor * plus + minus_factor * minus)
                 - cross_factor * energy * plus * minus
             )
@@ -494,7 +505,8 @@
             out[pl.ds(line, comps_local, stride=rows), :] = returned[line]
 
     for dg in range(1, group):
-        pltpu.make_async_copy(grids, gbuf.at[0], sem_grid_s.at[dg]).wait()
+        for i in range(3):
+            pltpu.make_async_copy(gbuf.at[0, i], gbuf.at[0, i], sem_grid_s.at[dg, i]).wait()
 
         @pl.loop(0, chunks)
         def _(ch):
@@ -531,8 +543,6 @@
     smem = pl.BlockSpec(memory_space=pltpu.SMEM)
     f32, bf16, i32 = jnp.float32, jnp.bfloat16, jnp.int32
     dma = pltpu.SemaphoreType.DMA
-    qi_rows = quad_index.transpose(0, 2, 1).reshape(8, comp_total)
-    qw_rows = quad_weight.transpose(0, 2, 1).reshape(8, comp_total)
     out = pl.pallas_call(
         functools.partial(step_kernel, nz, nx, nc),
         name="wave_step",
@@ -550,11 +560,12 @@
             pltpu.VMEM((2, comp_total, comp_total), bf16),
             pltpu.VMEM((comp_total, comp_total), bf16),
             pltpu.VMEM((comp_total, cols), f32),
+            pltpu.VMEM((comp_total, cols), f32),
             pltpu.VMEM((comp_total, cols), bf16),
             pltpu.VMEM((share, comp_total, cols), f32),
             pltpu.VMEM((rows, comps_local, cols), f32),
-            dma((group,)),
-            dma((group,)),
+            dma((group, 3)),
+            dma((group, 3)),
             dma((group, own // CHUNK)),
             dma((group, own // CHUNK)),
             dma((share,)),
@@ -567,14 +578,14 @@
         ),
     )(
         spectrum.reshape(comps_local * rows, cols),
-        jnp.stack([sea_mask, depth_class, current_class]),
-        coupling[:, None],
-        qi_rows.T,
-        qw_rows.T,
-        qi_rows,
-        qw_rows,
+        sea_mask,
+        depth_class,
+        current_class,
+        coupling.reshape(comp_total // TILE, TILE),
+        quad_index.transpose(0, 2, 1),
+        quad_weight.transpose(0, 2, 1),
         speed_table,
-        current_table,
+        current_table.T,
         turns,
     )
     return out.reshape(comps_local, rows, cols)
@@ -589,9 +600,10 @@
         comps_local % (nx * nc) == 0
         and own % NDIR == 0
         and own % CHUNK == 0
+        and CHUNK % BLOCK == 0
         and NDIR % BLOCK == 0
         and rows == 8
-        and cols % 128 == 0
+        and cols == TILE
         and rows % nz == 0
         and comp_total % TILE == 0
         and comps_local % 96 == 0

time: 83 us -> 70.9 us (0.85)
  local copies, waits for them, and re-layouts: 8.52 us -> 2.36 us
  Pallas kernels: 72.7 us -> 68.3 us
  other arithmetic: 1.31 us -> 0 us
    pallas_call x1, Pallas kernels: 72.7 us -> 68.3 us  [fused(): pl.pallas_call(functools.partial(step_kernel, nz, nx, nc), name='wave_ste...]
    transpose x2 -> x0, local copies, waits for them, and re-layouts: 2.19 us -> none  [fused(): out = pl.pallas_call(functools.partial(step_kernel, nz, nx, nc), name='wa...]
    reshape x2 -> x0, local copies, waits for them, and re-layouts: 1.58 us -> none  [the longest x1 0.8 us: fused(): qw_rows = quad_weight.transpose(0, 2, 1).reshape(8, comp_total)]
    unnamed x8 -> x1, local copies, waits for them, and re-layouts: 3.72 us -> 2.36 us
    another operation x1 -> x0, other arithmetic: 1.31 us -> none  [fused(): jnp.stack([sea_mask, depth_class, current_class])]
    broadcast_in_dim x1 -> x0, local copies, waits for them, and re-layouts: 1.03 us -> none  [fused(): coupling[:, None]]
where the time goes in v2:
time: 70.9 us; the launch traced here: 70.7 us
  Pallas kernels  68.3 us (96%)
  local copies, waits for them, and re-layouts  2.36 us (3%)
    pallas_call x1, Pallas kernels, fused(): pl.pallas_call(functools.partial(step_kernel, nz, nx, nc), name='wave_ste...  68.3 us
    unnamed x1, local copies, waits for them, and re-layouts  2.36 us

profile of v2, /device:TPU:19, one launch (start us, length us, event | category | flops | bytes accessed | tf_op | source)
XLA Modules:
  0.0 70.7 jit_solution(16392736767120115903)
XLA Ops:
  0.0 68.3 %wave_step.1 = f32[2304,128]{1,0:T(8,128)} custom-call(f32[2304,128]{1,0:T(8,128)} %bitcast.7, s32[8,128]{1,0:T(8,128)} %sea_mask.1, s32[8,128]{1,0:T(8,128)} %depth_class.1, s32[8,128]{1,0:T(8,128)} %current_class.1, f32[9,128]{1,0:T(8,128)} %bitcast.10, s32[2,4,1152]{2,1,0:T(4,128)} %bitcast.8, f32[2,4,1152]{2,1,0:T(4,128)} %bitcast.9, ...), custom_call_target="tpu_custom_call" | custom-call | tf_op jit(solution)/shard_map/wave_step/pallas_call | solution.py:546
  68.3 2.4 %copy.12 = f32[288,8,128]{2,1,0:T(8,128)} copy(f32[288,8,128]{2,1,0:T(8,128)} %bitcast.6) | data formatting | bytes 2359296

commit v3 on v2

--- a/solution.py
+++ b/solution.py
@@ -290,8 +290,8 @@
                     device_id_type=MESH,
                 ).start()
 
-    lanes = lax.broadcasted_iota(jnp.int32, (TILE, comp_total), 1)
-    subs = lax.broadcasted_iota(jnp.int32, (TILE, comp_total), 0)
+    lanes = lax.broadcasted_iota(jnp.int32, (TILE, TILE), 1)
+    subs = lax.broadcasted_iota(jnp.int32, (TILE, TILE), 0)
 
     def make_dense(t):
         start = aligned(t * TILE, TILE)
@@ -305,27 +305,30 @@
         )
         indices = indices.astype(jnp.int32)
         for side in range(2):
-            block = jnp.zeros((TILE, comp_total), jnp.float32)
-            for corner in range(4):
-                col = side * 4 + corner
-                block = jnp.where(
-                    lanes == indices[:, col : col + 1], weights[:, col : col + 1], block
-                )
-            kern[side, spot, :] = block.astype(jnp.bfloat16)
+            for left in range(0, comp_total, TILE):
+                block = jnp.zeros((TILE, TILE), jnp.float32)
+                for corner in range(4):
+                    one = slice(side * 4 + corner, side * 4 + corner + 1)
+                    block = jnp.where(lanes + left == indices[:, one], weights[:, one], block)
+                kern[side, spot, left : left + TILE] = block.astype(jnp.bfloat16)
 
     def make_dense_t(t):
         start = aligned(t * TILE, TILE)
         spot = pl.ds(start, TILE)
-        both = []
-        for side in range(2):
-            block = jnp.zeros((TILE, comp_total), jnp.float32)
-            for corner in range(4):
-                one = slice(corner, corner + 1)
-                block = jnp.where(
-                    subs + start == quad_index[side, one, :], quad_weight[side, one, :], block
-                )
-            both.append(block)
-        kern_t[spot, :] = (both[0] + both[1]).astype(jnp.bfloat16)
+        for left in range(0, comp_total, TILE):
+            part = slice(left, left + TILE)
+            both = []
+            for side in range(2):
+                block = jnp.zeros((TILE, TILE), jnp.float32)
+                for corner in range(4):
+                    one = slice(corner, corner + 1)
+                    block = jnp.where(
+                        subs + start == quad_index[side, one, part],
+                        quad_weight[side, one, part],
+                        block,
+                    )
+                both.append(block)
+            kern_t[spot, part] = (both[0] + both[1]).astype(jnp.bfloat16)
 
     for g in range(group):
         for i in range(3):

time: 70.9 us -> 70.9 us (level)
  no operation moved by 1% of the time
where the time goes in v3:
time: 70.9 us; the launch traced here: 70.7 us
  Pallas kernels  68.3 us (96%)
  local copies, waits for them, and re-layouts  2.36 us (3%)
    pallas_call x1, Pallas kernels, fused(): pl.pallas_call(functools.partial(step_kernel, nz, nx, nc), name='wave_ste...  68.3 us
    unnamed x1, local copies, waits for them, and re-layouts  2.36 us

profile of v3, /device:TPU:19, one launch (start us, length us, event | category | flops | bytes accessed | tf_op | source)
XLA Modules:
  0.0 70.7 jit_solution(10441169727353256243)
XLA Ops:
  0.0 68.3 %wave_step.1 = f32[2304,128]{1,0:T(8,128)} custom-call(f32[2304,128]{1,0:T(8,128)} %bitcast.7, s32[8,128]{1,0:T(8,128)} %sea_mask.1, s32[8,128]{1,0:T(8,128)} %depth_class.1, s32[8,128]{1,0:T(8,128)} %current_class.1, f32[9,128]{1,0:T(8,128)} %bitcast.10, s32[2,4,1152]{2,1,0:T(4,128)} %bitcast.8, f32[2,4,1152]{2,1,0:T(4,128)} %bitcast.9, ...), custom_call_target="tpu_custom_call" | custom-call | tf_op jit(solution)/shard_map/wave_step/pallas_call | solution.py:549
  68.3 2.4 %copy.12 = f32[288,8,128]{2,1,0:T(8,128)} copy(f32[288,8,128]{2,1,0:T(8,128)} %bitcast.6) | data formatting | bytes 2359296
